TPU v7x, 128 devices: a whole 4x4x4 slice. The times are simulated.
128 devices in a mesh: req: 32 (over y, z, core), grp: 4 (over x).
Axes of the slice: x: 4, y: 4, z: 4, core: 2. Of those that a mesh axis runs over, the one named last changes fastest.
Arguments:
- hidden_in: bfloat16 [16384, 2048], P('req'), may hold values from -6 to 6
- attn_gain: float32 [2048], replicated, may hold values from 0.1 to 1.9
- mlp_gain: float32 [2048], replicated, may hold values from 0.1 to 1.9
- w_query: bfloat16 [2048, 2048], P(None, 'grp'), may hold values from -0.75 to 0.75
- w_key: bfloat16 [2048, 512], P(None, 'grp'), may hold values from -0.125 to 0.125
- w_value: bfloat16 [2048, 512], P(None, 'grp'), may hold values from -0.125 to 0.125
- w_out: bfloat16 [2048, 2048], P('grp'), may hold values from -0.125 to 0.125
- w_gate: bfloat16 [2048, 8192], P(None, 'req'), may hold values from -0.125 to 0.125
- w_up: bfloat16 [2048, 8192], P(None, 'req'), may hold values from -0.125 to 0.125
- w_down: bfloat16 [8192, 2048], P('req'), may hold values from -0.0625 to 0.0625
- cache_k: bfloat16 [16384, 16, 512], P('req', None, 'grp'), may hold values from -4000 to 4000
- cache_v: bfloat16 [16384, 16, 512], P('req', None, 'grp'), may hold values from -6 to 6
- owner_of_row: int32 [16384], P('req'), may hold values from 0 to 31, as said below
- new_len: int32 [32, 32], P('req'), may hold values from 0 to 32, as said below
- prior_len: int32 [32, 32], P('req'), may hold values from 0 to 256, as said below
- page_table: int32 [32, 512], P('req'), may hold values from 0 to 511, each once within a row
Outputs:
- layer_out: bfloat16 [16384, 2048], P(('req', 'grp'))
- new_cache_k: bfloat16 [16384, 16, 512], P('req', None, 'grp')
- new_cache_v: bfloat16 [16384, 16, 512], P('req', None, 'grp')
Inputs may be any that keep to these rules, and one draw needn't show every extreme that they name: `owner_of_row`: rows of one block of 512 that name the same owner are consecutive; each block holds at most one request for each owner, of at most 32 rows; in every draw one owner receives a request of exactly 32 rows from every block. new_len[o, s] is the number of rows of block s of owner_of_row that name o. prior_len[o, s] + new_len[o, s] <= 256.
All inputs are finite; a program needn't handle non-finite values.
Results may differ from a plain program's by a relative error of at most 0.0063.
Values may be sent and summed in bfloat16 or wider, within the bound.
A program may use at most 128 MiB of HBM per device.

v0:
```python
import jax
import jax.numpy as jnp
from jax import lax
from jax.sharding import PartitionSpec as P

HD = 64
PAGE = 16
MAXP = 16
CONTEXT = 256
EPSILON = 1e-05
RESIDUAL_MULT = 0.22
SCORE_MULT = 0.015625
ROPE_BASE = 10000000.0


def normalize(values, gain):
    mean_square = jnp.mean(values * values, axis=-1, keepdims=True)
    return values * lax.rsqrt(mean_square + EPSILON) * gain


def rotary(values, positions):
    dim = values.shape[-1]
    half = dim // 2
    freq = jnp.power(ROPE_BASE, -2.0 * jnp.arange(half, dtype=jnp.int32).astype(jnp.float32) / dim)
    angle = positions.astype(jnp.float32)[:, :, None] * freq
    cosine = jnp.cos(angle)[:, :, None, :]
    sine = jnp.sin(angle)[:, :, None, :]
    first = values[..., :half].astype(jnp.float32)
    second = values[..., half:].astype(jnp.float32)
    return jnp.concatenate(
        [first * cosine - second * sine, second * cosine + first * sine], axis=-1
    )


def source_layout(owner_block, peers, pair_rows):
    row_count = owner_block.shape[0]
    owners = jnp.arange(peers, dtype=jnp.int32)
    member = owner_block[None, :] == owners[:, None]
    counts = jnp.sum(member.astype(jnp.int32), axis=1)
    row_ids = jnp.arange(row_count, dtype=jnp.int32)
    starts = jnp.min(jnp.where(member, row_ids[None, :], row_count), axis=1)
    slots = jnp.arange(pair_rows, dtype=jnp.int32)
    gather_rows = jnp.where(
        slots[None, :] < counts[:, None], starts[:, None] + slots[None, :], row_count
    )
    row_start = jnp.sum(jnp.where(member, starts[:, None], 0), axis=0)
    back_rows = owner_block * pair_rows + (row_ids - row_start)
    return (gather_rows.reshape(-1), back_rows)


def owner_attention(query_in, key_in, value_in, cache_keys, cache_values, lengths, priors, table):
    sources, pair_rows, qcols = query_in.shape
    kcols = key_in.shape[-1]
    kv_heads = kcols // HD
    group = qcols // kcols
    pool_pages = cache_keys.shape[0]
    slots = jnp.arange(pair_rows, dtype=jnp.int32)
    positions = priors[:, None] + slots[None, :]
    live = slots[None, :] < lengths[:, None]
    query_rot = rotary(query_in.reshape(sources, pair_rows, qcols // HD, HD), positions).astype(
        jnp.bfloat16
    )
    key_rot = rotary(key_in.reshape(sources, pair_rows, kv_heads, HD), positions).astype(
        jnp.bfloat16
    )
    key_rot = key_rot.reshape(sources, pair_rows, kcols)
    pages = table.reshape(sources, MAXP)
    page_index = jnp.minimum(positions // PAGE, MAXP - 1)
    target = jnp.take_along_axis(pages, page_index, axis=1)
    target = jnp.where(live, target, pool_pages).reshape(-1)
    offset = (positions % PAGE).reshape(-1)
    keys_out = cache_keys.at[target, offset].set(key_rot.reshape(-1, kcols), mode="drop")
    values_out = cache_values.at[target, offset].set(value_in.reshape(-1, kcols), mode="drop")
    key_block = jnp.take(keys_out, pages.reshape(-1), axis=0).reshape(
        sources, CONTEXT, kv_heads, HD
    )
    value_block = jnp.take(values_out, pages.reshape(-1), axis=0).reshape(
        sources, CONTEXT, kv_heads, HD
    )
    grouped = query_rot.reshape(sources, pair_rows, kv_heads, group, HD)
    scores = (
        jnp.einsum("stkgd,sjkd->skgtj", grouped, key_block, preferred_element_type=jnp.float32)
        * SCORE_MULT
    )
    allowed = (
        jnp.arange(CONTEXT, dtype=jnp.int32)[None, None, None, None, :]
        <= positions[:, None, None, :, None]
    )
    scores = jnp.where(allowed, scores, -jnp.inf)
    top = jnp.max(scores, axis=-1, keepdims=True)
    weights = jnp.exp(scores - top)
    probs = (weights / jnp.sum(weights, axis=-1, keepdims=True)).astype(jnp.bfloat16)
    mixed = jnp.einsum("skgtj,sjkd->stkgd", probs, value_block, preferred_element_type=jnp.float32)
    return (mixed.astype(jnp.bfloat16).reshape(sources, pair_rows, qcols), keys_out, values_out)


def body(
    hidden_in,
    attn_gain,
    mlp_gain,
    w_query,
    w_key,
    w_value,
    w_out,
    w_gate,
    w_up,
    w_down,
    cache_k,
    cache_v,
    owner_of_row,
    new_len,
    prior_len,
    page_table,
):
    peers = lax.axis_size("req")
    groups = lax.axis_size("grp")
    row_count = hidden_in.shape[0]
    pair_rows = 2 * row_count // peers
    quarter = row_count // groups
    group_index = lax.axis_index("grp")
    normed = normalize(hidden_in.astype(jnp.float32), attn_gain).astype(jnp.bfloat16)
    query_rows = jnp.dot(normed, w_query, preferred_element_type=jnp.float32).astype(jnp.bfloat16)
    key_rows = jnp.dot(normed, w_key, preferred_element_type=jnp.float32).astype(jnp.bfloat16)
    value_rows = jnp.dot(normed, w_value, preferred_element_type=jnp.float32).astype(jnp.bfloat16)
    gather_rows, back_rows = source_layout(owner_of_row, peers, pair_rows)
    send_query = jnp.take(query_rows, gather_rows, axis=0, mode="fill", fill_value=0).reshape(
        peers, pair_rows, -1
    )
    send_key = jnp.take(key_rows, gather_rows, axis=0, mode="fill", fill_value=0).reshape(
        peers, pair_rows, -1
    )
    send_value = jnp.take(value_rows, gather_rows, axis=0, mode="fill", fill_value=0).reshape(
        peers, pair_rows, -1
    )
    recv_query, recv_key, recv_value = (
        lax.all_to_all(send_query, "req", split_axis=0, concat_axis=0, tiled=True),
        lax.all_to_all(send_key, "req", split_axis=0, concat_axis=0, tiled=True),
        lax.all_to_all(send_value, "req", split_axis=0, concat_axis=0, tiled=True),
    )
    mixed, keys_out, values_out = owner_attention(
        recv_query, recv_key, recv_value, cache_k, cache_v, new_len[0], prior_len[0], page_table[0]
    )
    returned = lax.all_to_all(mixed, "req", split_axis=0, concat_axis=0, tiled=True)
    attn_rows = jnp.take(returned.reshape(peers * pair_rows, -1), back_rows, axis=0)
    projected = jnp.dot(attn_rows, w_out, preferred_element_type=jnp.float32)
    total = lax.psum(projected.astype(jnp.bfloat16), "grp").astype(jnp.float32)
    attn_part = lax.dynamic_slice_in_dim(total, group_index * quarter, quarter, 0)
    own_rows = lax.dynamic_slice_in_dim(hidden_in, group_index * quarter, quarter, 0).astype(
        jnp.float32
    )
    residual = own_rows + RESIDUAL_MULT * attn_part
    mlp_in = normalize(residual, mlp_gain).astype(jnp.bfloat16)
    piece = lax.all_gather(mlp_in, "req", axis=0, tiled=True)
    gate = jnp.dot(piece, w_gate, preferred_element_type=jnp.float32)
    upper = jnp.dot(piece, w_up, preferred_element_type=jnp.float32)
    hidden = (jax.nn.silu(gate) * upper).astype(jnp.bfloat16)
    down = lax.psum_scatter(
        jnp.dot(hidden, w_down, preferred_element_type=jnp.float32).astype(jnp.bfloat16),
        "req",
        scatter_dimension=0,
        tiled=True,
    ).astype(jnp.float32)
    layer_out = (residual + RESIDUAL_MULT * down).astype(jnp.bfloat16)
    return (layer_out, keys_out, values_out)


def solution(mesh):
    in_specs = (
        P("req", None),
        P(),
        P(),
        P(None, "grp"),
        P(None, "grp"),
        P(None, "grp"),
        P("grp", None),
        P(None, "req"),
        P(None, "req"),
        P("req", None),
        P("req", None, "grp"),
        P("req", None, "grp"),
        P("req"),
        P("req", None),
        P("req", None),
        P("req", None),
    )
    out_specs = (P(("req", "grp"), None), P("req", None, "grp"), P("req", None, "grp"))
    return jax.shard_map(body, mesh=mesh, in_specs=in_specs, out_specs=out_specs, check_vma=False)
```

profile of v0, /device:TPU:0, one launch (start us, length us, event | category | flops | bytes accessed | tf_op | source)
XLA Modules:
  0.0 475.2 jit_solution(9839665422419617770)
XLA Ops:
  7.2 3.4 copy.67
  18.9 3.2 gather_fusion.5
  22.1 3.2 gather_fusion.3
  26.3 8.4 %all-to-all-start.1 = ((bf16[32,32,128]{2,1,0:T(8,128)(2,1)}), bf16[32,32,128]{2,1,0:T(8,128)(2,1)S(1)}, u32[]{:S(2)}, u32[]{:S(2)}) async-start(bf16[32,32,128]{2,1,0:T(8,128)(2,1)} %bitcast.10), calls=%async_computation.1 | async-start | bytes 524288 | tf_op jit(solution)/shard_map/all_to_all | solution.py:137
  37.1 7.1 %gather_fusion.2 = s32[1024]{0:T(1024)S(1)} fusion(s32[32,16]{1,0:T(8,128)S(1)} %reshape_squeeze.3, s32[1024]{0:T(1024)S(1)} %reshape.573), kind=kCustom, calls=%fused_computation.6 | custom fusion | bytes 16384 | tf_op jit(solution)/shard_map/jit(take_along_axis)/gather | solution.py:69
  44.4 3.5 convolution_convert_fusion.2
  48.0 5.1 %gather_fusion = bf16[1024,512]{1,0:T(8,128)(2,1)} fusion(bf16[512,512]{1,0:T(8,128)(2,1)S(1)} %convolution_convert_fusion.2, s32[1024]{0:T(1024)S(1)} %broadcast_clamp_fusion), kind=kCustom, calls=%fused_computation.4 | custom fusion | bytes 2101248 | tf_op jit(solution)/shard_map/jit(_take)/gather | solution.py:126
  56.4 7.5 %all-to-all-start = ((bf16[32,32,128]{2,1,0:T(8,128)(2,1)}), bf16[32,32,128]{2,1,0:T(8,128)(2,1)}, u32[]{:S(2)}, u32[]{:S(2)}) async-start(bf16[32,32,128]{2,1,0:T(8,128)(2,1)} %bitcast.5), calls=%async_computation | async-start | bytes 524288 | tf_op jit(solution)/shard_map/all_to_all | solution.py:138
  63.9 2.9 multiply_cosine_fusion
  67.1 5.7 %all-to-all-done = bf16[32,32,128]{2,1,0:T(8,128)(2,1)} async-done(((bf16[32,32,128]{2,1,0:T(8,128)(2,1)}), bf16[32,32,128]{2,1,0:T(8,128)(2,1)}, u32[]{:S(2)}, u32[]{:S(2)}) %all-to-all-start) | async-done | bytes 262176 | tf_op jit(solution)/shard_map/all_to_all | solution.py:138
  72.9 5.1 %all-to-all-start.2 = ((bf16[32,32,512]{2,1,0:T(8,128)(2,1)}), bf16[32,32,512]{2,1,0:T(8,128)(2,1)}, u32[]{:S(2)}, u32[]{:S(2)}) async-start(bf16[32,32,512]{2,1,0:T(8,128)(2,1)} %broadcast_select_fusion.2), calls=%async_computation.2 | async-start | bytes 2097152 | tf_op jit(solution)/shard_map/all_to_all | solution.py:136
  81.6 6.5 %scatter_fusion.1 = bf16[8192,128]{1,0:T(8,128)(2,1)} fusion(bf16[8192,128]{1,0:T(8,128)(2,1)} %bitcast.52, s32[1024]{0:T(1024)S(1)} %broadcast_select_fusion.5, bf16[1024,128]{1,0:T(8,128)(2,1)S(1)} %reshape.587), kind=kCustom, calls=%fused_computation.8 | custom fusion | bytes 790528
  88.0 4.0 gather_fusion.6
  92.0 6.9 %scatter_fusion = bf16[8192,128]{1,0:T(8,128)(2,1)} fusion(bf16[8192,128]{1,0:T(8,128)(2,1)} %bitcast.49, s32[1024]{0:T(1024)S(1)} %broadcast_select_fusion.5, bf16[1024,128]{1,0:T(8,128)(2,1)} %bitcast.6), kind=kCustom, calls=%fused_computation.7 | custom fusion | bytes 790528
  98.9 4.0 gather_fusion.4
  102.9 4.6 broadcast_select_fusion.1
  107.5 8.2 %reshape.510 = bf16[32,256,2,64]{3,2,1,0:T(2,128)(2,1)} reshape(bf16[512,16,128]{2,1,0:T(8,128)(2,1)} %get-tuple-element.22) | data formatting | bytes 4194304 | tf_op jit(solution)/shard_map/reshape | solution.py:77
  115.7 8.3 %reshape.513 = bf16[32,256,2,64]{3,2,1,0:T(2,128)(2,1)} reshape(bf16[512,16,128]{2,1,0:T(8,128)(2,1)} %get-tuple-element.23) | data formatting | bytes 4194304 | tf_op jit(solution)/shard_map/reshape | solution.py:74
  124.0 3.9 reshape.514
  127.9 4.0 fusion.7
  135.8 4.9 %fusion.49 = (f32[32,2,4,32]{3,2,1,0:T(4,128)S(1)}, f32[32,2,4,32,256]{4,3,2,1,0:T(8,128)}) fusion(f32[32,2,256,32,4]{2,3,4,1,0:T(8,128)S(1)} %fusion.10, pred[32,32,256]{2,1,0:T(8,128)(4,1)S(1)} %copy-done.6), kind=kOutput, calls=%fused_computation.132 | output fusion | flops 12583167 | bytes 17072128 | tf_op jit(solution)/shard_map/sub | solution.py:91
  140.7 4.5 convert_bitcast_fusion
  147.7 4.7 reshape.515
  152.4 7.5 %all-to-all-start.3 = ((bf16[32,32,512]{2,1,0:T(8,128)(2,1)}), bf16[32,32,512]{2,1,0:T(8,128)(2,1)S(1)}, u32[]{:S(2)}, u32[]{:S(2)}) async-start(bf16[32,32,512]{2,1,0:T(8,128)(2,1)} %reshape.515), calls=%async_computation.3 | async-start | bytes 2097152 | tf_op jit(solution)/shard_map/all_to_all | solution.py:143
  159.9 16.7 %all-to-all-done.3 = bf16[32,32,512]{2,1,0:T(8,128)(2,1)S(1)} async-done(((bf16[32,32,512]{2,1,0:T(8,128)(2,1)}), bf16[32,32,512]{2,1,0:T(8,128)(2,1)S(1)}, u32[]{:S(2)}, u32[]{:S(2)}) %all-to-all-start.3) | async-done | bytes 1048608 | tf_op jit(solution)/shard_map/all_to_all | solution.py:143
  176.7 2.6 gather_fusion.1
  179.3 3.7 convolution_convert_fusion.1
  183.1 56.8 %all-reduce.2.cloned.1.call-done = bf16[512,2048]{1,0:T(8,128)(2,1)} async-done(((bf16[512,2048]{1,0:T(8,128)(2,1)}), bf16[512,2048]{1,0:T(8,128)(2,1)}) %all-reduce.2.cloned.1.call-update) | async-done | bytes 2097168 | tf_op jit(solution)/shard_map/psum | solution.py:146
  243.7 72.5 %all-gather.2.cloned.1.call-done = bf16[4096,2048]{1,0:T(8,128)(2,1)} async-done(((bf16[128,2048]{1,0:T(8,128)(2,1)}), bf16[4096,2048]{1,0:T(8,128)(2,1)}) %all-gather.2.cloned.1.call-update) | async-done | bytes 16777232 | tf_op jit(solution)/shard_map/all_gather | solution.py:153
  316.2 10.2 %fusion.50 = f32[4096,256]{1,0:T(8,128)} fusion(bf16[4096,2048]{1,0:T(8,128)(2,1)} %all-gather.2.cloned.1.call-done, bf16[2048,256]{1,0:T(8,128)(2,1)S(1)} %copy-done.14), kind=kOutput, calls=%fused_computation.133 | convolution fusion | flops 4294967296 | bytes 22020096 | tf_op jit(solution)/shard_map/dot_general | solution.py:154
  326.4 24.7 %convolution_convert_fusion = bf16[4096,2048]{1,0:T(8,128)(2,1)} fusion(bf16[256,2048]{1,0:T(8,128)(2,1)} %param.29, bf16[4096,2048]{1,0:T(8,128)(2,1)} %all-gather.2.cloned.1.call-done, bf16[2048,256]{1,0:T(8,128)(2,1)} %param.28, f32[4096,256]{1,0:T(8,128)} %fusion.50), kind=kOutput, calls=%fused_computation.10 | convolution fusion | flops 8604614656 | bytes 39845888 | tf_op jit(solution)/shard_map/dot_general | solution.py:158
  351.2 114.9 %reduce-scatter.2.cloned.1.call-done = bf16[128,2048]{1,0:T(8,128)(2,1)} async-done(((bf16[4096,2048]{1,0:T(8,128)(2,1)}), bf16[128,2048]{1,0:T(8,128)(2,1)}) %reduce-scatter.2.cloned.1.call-update) | async-done | bytes 524304 | tf_op jit(solution)/shard_map/reduce_scatter | solution.py:157
  (100 shorter events, 31.5 us)
Async XLA Ops:
  7.2 172.1 %copy-start = (bf16[512,2048]{1,0:T(8,128)(2,1)S(1)}, bf16[512,2048]{1,0:T(8,128)(2,1)}, u32[]{:S(2)}) copy-start(bf16[512,2048]{1,0:T(8,128)(2,1)} %param.26) | copy-start | bytes 6291460
  7.2 3.4 copy-start.5
  7.2 4.8 %copy-start.8 = (s32[512]{0:T(512)S(1)}, s32[512]{0:T(512)}, u32[]{:S(2)}) copy-start(s32[512]{0:T(512)} %param.32) | copy-start | bytes 6148
  10.6 4.0 copy-start.15
  10.6 4.0 copy-start.16
  12.3 4.6 copy-start.2
  18.8 15.9 %copy-start.7 = (s32[1,512]{1,0:T(1,128)S(1)}, s32[1,512]{1,0:T(1,128)}, u32[]{:S(2)}) copy-start(s32[1,512]{1,0:T(1,128)} %param.35) | copy-start | bytes 6148
  18.8 16.0 %copy-start.10 = (s32[1,32]{1,0:T(1,128)S(1)}, s32[1,32]{1,0:T(1,128)}, u32[]{:S(2)}) copy-start(s32[1,32]{1,0:T(1,128)} %param.34) | copy-start | bytes 388
  18.8 17.6 %copy-start.11 = (s32[1,32]{1,0:T(1,128)S(1)}, s32[1,32]{1,0:T(1,128)}, u32[]{:S(2)}) copy-start(s32[1,32]{1,0:T(1,128)} %param.33) | copy-start | bytes 388
  26.3 30.1 %all-to-all-start.1 = ((bf16[32,32,128]{2,1,0:T(8,128)(2,1)}), bf16[32,32,128]{2,1,0:T(8,128)(2,1)S(1)}, u32[]{:S(2)}, u32[]{:S(2)}) async-start(bf16[32,32,128]{2,1,0:T(8,128)(2,1)} %bitcast.10), calls=%async_computation.1 | async-start | bytes 524288 | tf_op jit(solution)/shard_map/all_to_all | solution.py:137
  37.1 7.2 %copy-start.13 = (s32[2]{0:T(128)S(1)}, s32[2]{0:T(128)}, u32[]{:S(2)}) copy-start(s32[2]{0:T(128)} %constant.139) | copy-start | bytes 28
  37.1 7.3 %copy-start.12 = (s32[2]{0:T(128)S(1)}, s32[2]{0:T(128)}, u32[]{:S(2)}) copy-start(s32[2]{0:T(128)} %constant.136) | copy-start | bytes 28
  56.4 16.4 %all-to-all-start = ((bf16[32,32,128]{2,1,0:T(8,128)(2,1)}), bf16[32,32,128]{2,1,0:T(8,128)(2,1)}, u32[]{:S(2)}, u32[]{:S(2)}) async-start(bf16[32,32,128]{2,1,0:T(8,128)(2,1)} %bitcast.5), calls=%async_computation | async-start | bytes 524288 | tf_op jit(solution)/shard_map/all_to_all | solution.py:138
  72.9 51.2 %all-to-all-start.2 = ((bf16[32,32,512]{2,1,0:T(8,128)(2,1)}), bf16[32,32,512]{2,1,0:T(8,128)(2,1)}, u32[]{:S(2)}, u32[]{:S(2)}) async-start(bf16[32,32,512]{2,1,0:T(8,128)(2,1)} %broadcast_select_fusion.2), calls=%async_computation.2 | async-start | bytes 2097152 | tf_op jit(solution)/shard_map/all_to_all | solution.py:136
  115.7 12.2 %copy-start.3 = (f32[32,32,32]{2,1,0:T(8,128)S(1)}, f32[32,32,32]{2,1,0:T(8,128)}, u32[]{:S(2)}) copy-start(f32[32,32,32]{2,1,0:T(8,128)} %get-tuple-element.16) | copy-start | bytes 393220
  131.9 2.2 copy-start.1
  134.1 1.7 copy-start.6
  135.8 4.9 %copy-start.4 = (bf16[32,256,2,64]{3,2,1,0:T(2,128)(2,1)S(1)}, bf16[32,256,2,64]{3,2,1,0:T(2,128)(2,1)}, u32[]{:S(2)}) copy-start(bf16[32,256,2,64]{3,2,1,0:T(2,128)(2,1)} %reshape.510) | copy-start | bytes 6291460
  152.4 24.3 %all-to-all-start.3 = ((bf16[32,32,512]{2,1,0:T(8,128)(2,1)}), bf16[32,32,512]{2,1,0:T(8,128)(2,1)S(1)}, u32[]{:S(2)}, u32[]{:S(2)}) async-start(bf16[32,32,512]{2,1,0:T(8,128)(2,1)} %reshape.515), calls=%async_computation.3 | async-start | bytes 2097152 | tf_op jit(solution)/shard_map/all_to_all | solution.py:143
  159.8 80.0 %all-reduce.2.cloned.1.call-start = ((), (), s32[]{:S(2)}) async-start(), calls=%async_computation.5 | async-start | bytes 4194304 | tf_op jit(solution)/shard_map/psum | solution.py:146
  179.3 62.1 %copy-start.9 = (f32[2048]{0:T(1024)S(1)}, f32[2048]{0:T(1024)}, u32[]{:S(2)}) copy-start(f32[2048]{0:T(1024)} %param.22) | copy-start | bytes 24580
  183.0 133.2 %copy-start.14 = (bf16[2048,256]{1,0:T(8,128)(2,1)S(1)}, bf16[2048,256]{1,0:T(8,128)(2,1)}, u32[]{:S(2)}) copy-start(bf16[2048,256]{1,0:T(8,128)(2,1)} %param.27) | copy-start | bytes 3145732
  183.0 133.2 %all-gather.2.cloned.1.call-start = ((), (), s32[]{:S(2)}) async-start(), calls=%async_computation.6 | async-start | bytes 17301504 | tf_op jit(solution)/shard_map/all_gather | solution.py:153
  243.6 222.4 %reduce-scatter.2.cloned.1.call-start = ((), (), s32[]{:S(2)}) async-start(), calls=%async_computation.7 | async-start | bytes 17301504 | tf_op jit(solution)/shard_map/reduce_scatter | solution.py:157
Sparse Core Ops, SparseCore 0:
  183.1 56.6 all-reduce.1
  243.8 72.4 all-gather.1
  351.3 114.7 reduce-scatter.1
where the time goes:
time: 482 us; the launch traced here: 475 us
  waiting for transfers between devices  267 us (55%)
  local copies, waits for them, and re-layouts  80.5 us (17%)
  matrix products  52.5 us (11%)
  other arithmetic  32.4 us (7%)
  starting transfers between devices  28.7 us (6%)
  between operations  14.4 us (3%)
    reduce_scatter x1, waiting for transfers between devices, body(): lax.psum_scatter(jnp.dot(hidden, w_down, preferred_element_type=jnp.float...  115 us
    all_gather x1, waiting for transfers between devices, body(): piece = lax.all_gather(mlp_in, 'req', axis=0, tiled=True)  72.5 us
    psum x1, waiting for transfers between devices, body(): total = lax.psum(projected.astype(jnp.bfloat16), 'grp').astype(jnp.float32)  56.8 us
    dot_general x1, matrix products, body(): jnp.dot(hidden, w_down, preferred_element_type=jnp.float32)  24.7 us
    unnamed x39, local copies, waits for them, and re-layouts  19.9 us
    all_to_all x1, waiting for transfers between devices, body(): lax.all_to_all(mixed, 'req', split_axis=0, concat_axis=0, tiled=True)  16.7 us
    dot_general x1, matrix products, body(): gate = jnp.dot(piece, w_gate, preferred_element_type=jnp.float32)  10.2 us
  transfers between devices with their start and end apart: 7, of which 5 were waited for; matrix products, arithmetic and copies ran while one was open for 15% of the time, Pallas kernels for 0%

commit v1 on v0

--- a/solution.py
+++ b/solution.py
@@ -143,7 +143,9 @@
     returned = lax.all_to_all(mixed, "req", split_axis=0, concat_axis=0, tiled=True)
     attn_rows = jnp.take(returned.reshape(peers * pair_rows, -1), back_rows, axis=0)
     projected = jnp.dot(attn_rows, w_out, preferred_element_type=jnp.float32)
-    total = lax.psum(projected.astype(jnp.bfloat16), "grp").astype(jnp.float32)
+    total = jnp.sum(lax.all_gather(projected.astype(jnp.bfloat16), "grp"), axis=0).astype(
+        jnp.float32
+    )
     attn_part = lax.dynamic_slice_in_dim(total, group_index * quarter, quarter, 0)
     own_rows = lax.dynamic_slice_in_dim(hidden_in, group_index * quarter, quarter, 0).astype(
         jnp.float32

time: 482 us -> 516 us (1.071)
  waiting for transfers between devices: 267 us -> 292 us
  other arithmetic: 32.4 us -> 39.6 us
    all_gather x0 -> x1, waiting for transfers between devices: none -> 81.3 us  [body(): lax.all_gather(projected.astype(jnp.bfloat16), 'grp')]
    psum x1 -> x0, waiting for transfers between devices: 56.8 us -> none  [body(): total = lax.psum(projected.astype(jnp.bfloat16), 'grp').astype(jnp.float32)]
    reduce_sum x0 -> x1, other arithmetic: none -> 7.24 us  [body(): jnp.sum(lax.all_gather(projected.astype(jnp.bfloat16), 'grp'), axis=0)]
  transfers between devices with their start and end apart: 7 -> 7, of which waited for: 5 -> 5; matrix products, arithmetic and copies ran while one was open for 15% -> 14% of each run, Pallas kernels for 0% -> 0%
where the time goes in v1:
time: 516 us; the launch traced here: 509 us
  waiting for transfers between devices  292 us (57%)
  local copies, waits for them, and re-layouts  80.5 us (16%)
  matrix products  52.7 us (10%)
  other arithmetic  39.6 us (8%)
  starting transfers between devices  28.7 us (6%)
  between operations  14.6 us (3%)
    reduce_scatter x1, waiting for transfers between devices, body(): lax.psum_scatter(jnp.dot(hidden, w_down, preferred_element_type=jnp.float...  115 us
    all_gather x1, waiting for transfers between devices, body(): lax.all_gather(projected.astype(jnp.bfloat16), 'grp')  81.3 us
    all_gather x1, waiting for transfers between devices, body(): piece = lax.all_gather(mlp_in, 'req', axis=0, tiled=True)  73.7 us
    dot_general x1, matrix products, body(): jnp.dot(hidden, w_down, preferred_element_type=jnp.float32)  24.7 us
    unnamed x39, local copies, waits for them, and re-layouts  19.9 us
    all_to_all x1, waiting for transfers between devices, body(): lax.all_to_all(mixed, 'req', split_axis=0, concat_axis=0, tiled=True)  16.7 us
    dot_general x1, matrix products, body(): gate = jnp.dot(piece, w_gate, preferred_element_type=jnp.float32)  10.4 us
  transfers between devices with their start and end apart: 7, of which 5 were waited for; matrix products, arithmetic and copies ran while one was open for 14% of the time, Pallas kernels for 0%

profile of v1, /device:TPU:0, one launch (start us, length us, event | category | flops | bytes accessed | tf_op | source)
XLA Modules:
  0.0 508.6 jit_solution(1393007268671180222)
XLA Ops:
  7.2 3.4 copy.66
  18.9 3.2 gather_fusion.5
  22.1 3.2 gather_fusion.3
  26.3 8.4 %all-to-all-start.1 = ((bf16[32,32,128]{2,1,0:T(8,128)(2,1)}), bf16[32,32,128]{2,1,0:T(8,128)(2,1)S(1)}, u32[]{:S(2)}, u32[]{:S(2)}) async-start(bf16[32,32,128]{2,1,0:T(8,128)(2,1)} %bitcast.10), calls=%async_computation.1 | async-start | bytes 524288 | tf_op jit(solution)/shard_map/all_to_all | solution.py:137
  37.1 7.1 %gather_fusion.2 = s32[1024]{0:T(1024)S(1)} fusion(s32[32,16]{1,0:T(8,128)S(1)} %reshape_squeeze.3, s32[1024]{0:T(1024)S(1)} %reshape.573), kind=kCustom, calls=%fused_computation.6 | custom fusion | bytes 16384 | tf_op jit(solution)/shard_map/jit(take_along_axis)/gather | solution.py:69
  44.4 3.5 convolution_convert_fusion.2
  48.0 5.1 gather_fusion
  56.4 7.5 %all-to-all-start = ((bf16[32,32,128]{2,1,0:T(8,128)(2,1)}), bf16[32,32,128]{2,1,0:T(8,128)(2,1)}, u32[]{:S(2)}, u32[]{:S(2)}) async-start(bf16[32,32,128]{2,1,0:T(8,128)(2,1)} %bitcast.5), calls=%async_computation | async-start | bytes 524288 | tf_op jit(solution)/shard_map/all_to_all | solution.py:138
  63.9 2.9 multiply_cosine_fusion
  67.1 5.7 %all-to-all-done = bf16[32,32,128]{2,1,0:T(8,128)(2,1)} async-done(((bf16[32,32,128]{2,1,0:T(8,128)(2,1)}), bf16[32,32,128]{2,1,0:T(8,128)(2,1)}, u32[]{:S(2)}, u32[]{:S(2)}) %all-to-all-start) | async-done | bytes 262176 | tf_op jit(solution)/shard_map/all_to_all | solution.py:138
  72.9 5.1 %all-to-all-start.2 = ((bf16[32,32,512]{2,1,0:T(8,128)(2,1)}), bf16[32,32,512]{2,1,0:T(8,128)(2,1)}, u32[]{:S(2)}, u32[]{:S(2)}) async-start(bf16[32,32,512]{2,1,0:T(8,128)(2,1)} %broadcast_select_fusion.2), calls=%async_computation.2 | async-start | bytes 2097152 | tf_op jit(solution)/shard_map/all_to_all | solution.py:136
  81.6 6.5 %scatter_fusion.1 = bf16[8192,128]{1,0:T(8,128)(2,1)} fusion(bf16[8192,128]{1,0:T(8,128)(2,1)} %bitcast.53, s32[1024]{0:T(1024)S(1)} %broadcast_select_fusion.5, bf16[1024,128]{1,0:T(8,128)(2,1)S(1)} %reshape.587), kind=kCustom, calls=%fused_computation.8 | custom fusion | bytes 790528
  88.0 4.0 gather_fusion.6
  92.0 6.9 %scatter_fusion = bf16[8192,128]{1,0:T(8,128)(2,1)} fusion(bf16[8192,128]{1,0:T(8,128)(2,1)} %bitcast.50, s32[1024]{0:T(1024)S(1)} %broadcast_select_fusion.5, bf16[1024,128]{1,0:T(8,128)(2,1)} %bitcast.6), kind=kCustom, calls=%fused_computation.7 | custom fusion | bytes 790528
  98.9 4.0 gather_fusion.4
  102.9 4.6 broadcast_select_fusion.1
  107.5 8.2 %reshape.510 = bf16[32,256,2,64]{3,2,1,0:T(2,128)(2,1)} reshape(bf16[512,16,128]{2,1,0:T(8,128)(2,1)} %get-tuple-element.22) | data formatting | bytes 4194304 | tf_op jit(solution)/shard_map/reshape | solution.py:77
  115.7 8.3 %reshape.513 = bf16[32,256,2,64]{3,2,1,0:T(2,128)(2,1)} reshape(bf16[512,16,128]{2,1,0:T(8,128)(2,1)} %get-tuple-element.23) | data formatting | bytes 4194304 | tf_op jit(solution)/shard_map/reshape | solution.py:74
  124.0 3.9 reshape.514
  127.9 4.0 fusion.7
  135.8 4.9 fusion.49
  140.7 4.5 convert_bitcast_fusion
  147.7 4.7 reshape.515
  152.4 7.5 %all-to-all-start.3 = ((bf16[32,32,512]{2,1,0:T(8,128)(2,1)}), bf16[32,32,512]{2,1,0:T(8,128)(2,1)S(1)}, u32[]{:S(2)}, u32[]{:S(2)}) async-start(bf16[32,32,512]{2,1,0:T(8,128)(2,1)} %reshape.515), calls=%async_computation.3 | async-start | bytes 2097152 | tf_op jit(solution)/shard_map/all_to_all | solution.py:143
  159.9 16.7 %all-to-all-done.3 = bf16[32,32,512]{2,1,0:T(8,128)(2,1)S(1)} async-done(((bf16[32,32,512]{2,1,0:T(8,128)(2,1)}), bf16[32,32,512]{2,1,0:T(8,128)(2,1)S(1)}, u32[]{:S(2)}, u32[]{:S(2)}) %all-to-all-start.3) | async-done | bytes 1048608 | tf_op jit(solution)/shard_map/all_to_all | solution.py:143
  179.3 3.7 convolution_convert_fusion.1
  183.1 81.3 %all-gather.6.cloned.1.call-done = bf16[2048,2048]{1,0:T(8,128)(2,1)} async-done(((bf16[512,2048]{1,0:T(8,128)(2,1)}), bf16[2048,2048]{1,0:T(8,128)(2,1)}) %all-gather.6.cloned.1.call-update) | async-done | bytes 8388624 | tf_op jit(solution)/shard_map/all_gather | solution.py:146
  264.4 7.2 %reduce_sum.61 = bf16[512,2048]{1,0:T(8,128)(2,1)} reduce(bf16[4,512,2048]{2,1,0:T(8,128)(2,1)} %bitcast.57, bf16[]{:T(256)} %constant.128.clone.1), dimensions={0}, to_apply=%region_8.11 | reduce | flops 3145728 | bytes 10485762 | tf_op jit(solution)/shard_map/reduce_sum | solution.py:146
  275.4 73.7 %all-gather.4.cloned.1.call-done = bf16[4096,2048]{1,0:T(8,128)(2,1)} async-done(((bf16[128,2048]{1,0:T(8,128)(2,1)}), bf16[4096,2048]{1,0:T(8,128)(2,1)}) %all-gather.4.cloned.1.call-update) | async-done | bytes 16777232 | tf_op jit(solution)/shard_map/all_gather | solution.py:155
  349.1 10.4 %fusion.50 = f32[4096,256]{1,0:T(8,128)} fusion(bf16[4096,2048]{1,0:T(8,128)(2,1)} %all-gather.4.cloned.1.call-done, bf16[2048,256]{1,0:T(8,128)(2,1)S(1)} %copy-done.14), kind=kOutput, calls=%fused_computation.133 | convolution fusion | flops 4294967296 | bytes 22020096 | tf_op jit(solution)/shard_map/dot_general | solution.py:156
  359.5 24.7 %convolution_convert_fusion = bf16[4096,2048]{1,0:T(8,128)(2,1)} fusion(bf16[256,2048]{1,0:T(8,128)(2,1)} %param.29, bf16[4096,2048]{1,0:T(8,128)(2,1)} %all-gather.4.cloned.1.call-done, bf16[2048,256]{1,0:T(8,128)(2,1)} %param.28, f32[4096,256]{1,0:T(8,128)} %fusion.50), kind=kOutput, calls=%fused_computation.10 | convolution fusion | flops 8604614656 | bytes 39845888 | tf_op jit(solution)/shard_map/dot_general | solution.py:160
  384.3 114.9 %reduce-scatter.2.cloned.1.call-done = bf16[128,2048]{1,0:T(8,128)(2,1)} async-done(((bf16[4096,2048]{1,0:T(8,128)(2,1)}), bf16[128,2048]{1,0:T(8,128)(2,1)}) %reduce-scatter.2.cloned.1.call-update) | async-done | bytes 524304 | tf_op jit(solution)/shard_map/reduce_scatter | solution.py:159
  (101 shorter events, 34.1 us)
Async XLA Ops:
  7.2 172.1 %copy-start = (bf16[512,2048]{1,0:T(8,128)(2,1)S(1)}, bf16[512,2048]{1,0:T(8,128)(2,1)}, u32[]{:S(2)}) copy-start(bf16[512,2048]{1,0:T(8,128)(2,1)} %param.26) | copy-start | bytes 6291460
  7.2 3.4 copy-start.5
  7.2 4.8 copy-start.8
  10.6 4.0 copy-start.15
  10.6 4.0 copy-start.16
  12.3 4.6 copy-start.2
  18.8 15.9 %copy-start.7 = (s32[1,512]{1,0:T(1,128)S(1)}, s32[1,512]{1,0:T(1,128)}, u32[]{:S(2)}) copy-start(s32[1,512]{1,0:T(1,128)} %param.35) | copy-start | bytes 6148
  18.8 16.0 %copy-start.10 = (s32[1,32]{1,0:T(1,128)S(1)}, s32[1,32]{1,0:T(1,128)}, u32[]{:S(2)}) copy-start(s32[1,32]{1,0:T(1,128)} %param.34) | copy-start | bytes 388
  18.8 17.6 %copy-start.11 = (s32[1,32]{1,0:T(1,128)S(1)}, s32[1,32]{1,0:T(1,128)}, u32[]{:S(2)}) copy-start(s32[1,32]{1,0:T(1,128)} %param.33) | copy-start | bytes 388
  26.3 30.1 %all-to-all-start.1 = ((bf16[32,32,128]{2,1,0:T(8,128)(2,1)}), bf16[32,32,128]{2,1,0:T(8,128)(2,1)S(1)}, u32[]{:S(2)}, u32[]{:S(2)}) async-start(bf16[32,32,128]{2,1,0:T(8,128)(2,1)} %bitcast.10), calls=%async_computation.1 | async-start | bytes 524288 | tf_op jit(solution)/shard_map/all_to_all | solution.py:137
  37.1 7.2 %copy-start.13 = (s32[2]{0:T(128)S(1)}, s32[2]{0:T(128)}, u32[]{:S(2)}) copy-start(s32[2]{0:T(128)} %constant.140) | copy-start | bytes 28
  37.1 7.3 %copy-start.12 = (s32[2]{0:T(128)S(1)}, s32[2]{0:T(128)}, u32[]{:S(2)}) copy-start(s32[2]{0:T(128)} %constant.137) | copy-start | bytes 28
  56.4 16.4 %all-to-all-start = ((bf16[32,32,128]{2,1,0:T(8,128)(2,1)}), bf16[32,32,128]{2,1,0:T(8,128)(2,1)}, u32[]{:S(2)}, u32[]{:S(2)}) async-start(bf16[32,32,128]{2,1,0:T(8,128)(2,1)} %bitcast.5), calls=%async_computation | async-start | bytes 524288 | tf_op jit(solution)/shard_map/all_to_all | solution.py:138
  72.9 51.2 %all-to-all-start.2 = ((bf16[32,32,512]{2,1,0:T(8,128)(2,1)}), bf16[32,32,512]{2,1,0:T(8,128)(2,1)}, u32[]{:S(2)}, u32[]{:S(2)}) async-start(bf16[32,32,512]{2,1,0:T(8,128)(2,1)} %broadcast_select_fusion.2), calls=%async_computation.2 | async-start | bytes 2097152 | tf_op jit(solution)/shard_map/all_to_all | solution.py:136
  115.7 12.2 %copy-start.3 = (f32[32,32,32]{2,1,0:T(8,128)S(1)}, f32[32,32,32]{2,1,0:T(8,128)}, u32[]{:S(2)}) copy-start(f32[32,32,32]{2,1,0:T(8,128)} %get-tuple-element.16) | copy-start | bytes 393220
  131.9 2.2 copy-start.1
  134.1 1.7 copy-start.6
  135.8 4.9 copy-start.4
  152.4 24.3 %all-to-all-start.3 = ((bf16[32,32,512]{2,1,0:T(8,128)(2,1)}), bf16[32,32,512]{2,1,0:T(8,128)(2,1)S(1)}, u32[]{:S(2)}, u32[]{:S(2)}) async-start(bf16[32,32,512]{2,1,0:T(8,128)(2,1)} %reshape.515), calls=%async_computation.3 | async-start | bytes 2097152 | tf_op jit(solution)/shard_map/all_to_all | solution.py:143
  159.8 104.5 %all-gather.6.cloned.1.call-start = ((), (), s32[]{:S(2)}) async-start(), calls=%async_computation.7 | async-start | bytes 10485760 | tf_op jit(solution)/shard_map/all_gather | solution.py:146
  183.0 166.1 %all-gather.4.cloned.1.call-start = ((), (), s32[]{:S(2)}) async-start(), calls=%async_computation.5 | async-start | bytes 17301504 | tf_op jit(solution)/shard_map/all_gather | solution.py:155
  264.4 8.7 %copy-start.9 = (f32[2048]{0:T(1024)S(1)}, f32[2048]{0:T(1024)}, u32[]{:S(2)}) copy-start(f32[2048]{0:T(1024)} %param.22) | copy-start | bytes 24580
  264.4 84.7 %copy-start.14 = (bf16[2048,256]{1,0:T(8,128)(2,1)S(1)}, bf16[2048,256]{1,0:T(8,128)(2,1)}, u32[]{:S(2)}) copy-start(bf16[2048,256]{1,0:T(8,128)(2,1)} %param.27) | copy-start | bytes 3145732
  275.4 223.8 %reduce-scatter.2.cloned.1.call-start = ((), (), s32[]{:S(2)}) async-start(), calls=%async_computation.6 | async-start | bytes 17301504 | tf_op jit(solution)/shard_map/reduce_scatter | solution.py:159
Sparse Core Ops, SparseCore 0:
  183.1 81.1 all-gather.5
  275.5 73.5 all-gather.3
  384.4 114.7 reduce-scatter.1
